TPU v7x, 32 devices: a whole 2x2x4 slice. The times are simulated.
32 devices in a mesh: groups: 2 (over y), role: 4 (over x, core), tp: 4 (over z).
Axes of the slice: x: 2, y: 2, z: 4, core: 2. Of those that a mesh axis runs over, the one named last changes fastest.
Arguments:
- x_teacher: bfloat16 [512, 8192], P('groups', 'tp'), parts along dimension 0, may hold values from -6 to 6
- x_student: bfloat16 [512, 4096], P('groups', 'role'), parts along dimension 0, may hold values from -6 to 6
- t_gate: bfloat16 [8192, 14336], P('tp', 'role'), may hold values from -0.0625 to 0.0625
- t_up: bfloat16 [8192, 14336], P('tp', 'role'), may hold values from -0.0625 to 0.0625
- t_down: bfloat16 [14336, 8192], P('role', 'tp'), may hold values from -0.046875 to 0.046875
- s_gate: bfloat16 [4096, 8192], P('role', 'tp'), may hold values from -0.09375 to 0.09375
- s_up: bfloat16 [4096, 8192], P('role', 'tp'), may hold values from -0.09375 to 0.09375
- s_down: bfloat16 [8192, 4096], P('tp', 'role'), may hold values from -0.0625 to 0.0625
- align: bfloat16 [4096, 8192], P('role', 'tp'), may hold values from -0.09375 to 0.09375
Outputs:
- grad_s_gate: bfloat16 [8192, 8192], P(('groups', 'role'), 'tp'), parts along dimension 0
- grad_s_up: bfloat16 [8192, 8192], P(('groups', 'role'), 'tp'), parts along dimension 0
- grad_s_down: bfloat16 [16384, 4096], P(('groups', 'tp'), 'role'), parts along dimension 0
- grad_align: bfloat16 [8192, 8192], P(('groups', 'role'), 'tp'), parts along dimension 0
There are 2 independent parts, one for each index of `groups`. A program takes and returns all parts, laid end to end along the dimension named above; an argument that names none is the same for every part. Nothing has to cross between parts.
All inputs are finite; a program needn't handle non-finite values.
Results may differ from a plain program's by a relative error of at most 0.009.
Values may be sent and summed in bfloat16 or wider, within the bound.
No kernel may reach another device: no remote copies, remote signals or barrier semaphores. Data moves between devices by JAX's collectives and lax.ppermute only.
A program may use at most 128 MiB of HBM per device.

v0:
```python
import jax
import jax.numpy as jnp
from jax import lax
from jax.sharding import PartitionSpec as P

loss_scale = 16.0


def contract_rows(left, right):
    return lax.dot_general(
        left, right, (((0,), (0,)), ((), ())), preferred_element_type=jnp.float32
    )


def contract_cols(left, right):
    return lax.dot_general(
        left, right, (((1,), (1,)), ((), ())), preferred_element_type=jnp.float32
    )


def role_sums(values):
    return lax.psum(values, "role")


def tp_sums(values):
    return lax.psum(values, "tp")


def tp_scatter(term_fn, share_rows):
    return lax.psum_scatter(
        term_fn(jnp.int32(0), lax.axis_size("tp") * share_rows),
        "tp",
        scatter_dimension=0,
        tiled=True,
    )


def tp_gather(shares, piece_fn):
    return piece_fn(lax.all_gather(shares, "tp", axis=0, tiled=True), jnp.int32(0))


def on_device(x_teacher, x_student, t_gate, t_up, t_down, s_gate, s_up, s_down, align):
    token_count = x_teacher.shape[0]
    unit_count = t_gate.shape[1]
    tp_devices = lax.axis_size("tp")

    def token_term(first_row, row_count):
        gate_rows = jnp.dot(x_teacher, t_gate, preferred_element_type=jnp.float32)
        up_rows = jnp.dot(x_teacher, t_up, preferred_element_type=jnp.float32)
        return jnp.concatenate([gate_rows, up_rows], axis=1)

    def project_rows(part_rows, first_row):
        return jnp.dot(part_rows, t_down, preferred_element_type=jnp.float32)

    shares = tp_scatter(token_term, token_count // tp_devices)
    hidden_share = (jax.nn.silu(shares[:, :unit_count]) * shares[:, unit_count:]).astype(
        jnp.bfloat16
    )
    features_part = tp_gather(hidden_share, project_rows)
    student_gate_part = jnp.dot(x_student, s_gate, preferred_element_type=jnp.float32)
    student_up_part = jnp.dot(x_student, s_up, preferred_element_type=jnp.float32)
    student_gate, student_up = role_sums((student_gate_part, student_up_part))
    gate_sigmoid = jax.nn.sigmoid(student_gate)
    gate_active = student_gate * gate_sigmoid
    student_hidden = (gate_active * student_up).astype(jnp.bfloat16)
    student_out = tp_sums(
        jnp.dot(student_hidden, s_down, preferred_element_type=jnp.float32)
    ).astype(jnp.bfloat16)
    aligned_part = jnp.dot(student_out, align, preferred_element_type=jnp.float32)
    difference = role_sums(aligned_part - features_part)
    grad_aligned = (difference * (2.0 * loss_scale / token_count)).astype(jnp.bfloat16)
    grad_align = contract_rows(student_out, grad_aligned).astype(jnp.bfloat16)
    grad_student_out = tp_sums(contract_cols(grad_aligned, align)).astype(jnp.bfloat16)
    grad_s_down = contract_rows(student_hidden, grad_student_out).astype(jnp.bfloat16)
    grad_hidden = role_sums(contract_cols(grad_student_out, s_down))
    slope = gate_sigmoid * (1.0 + student_gate * (1.0 - gate_sigmoid))
    grad_gate_pre = (grad_hidden * student_up * slope).astype(jnp.bfloat16)
    grad_up_pre = (grad_hidden * gate_active).astype(jnp.bfloat16)
    grad_s_gate = contract_rows(x_student, grad_gate_pre).astype(jnp.bfloat16)
    grad_s_up = contract_rows(x_student, grad_up_pre).astype(jnp.bfloat16)
    return (grad_s_gate, grad_s_up, grad_s_down, grad_align)


def solution(mesh):
    placed = (
        P("groups", "tp"),
        P("groups", "role"),
        P("tp", "role"),
        P("tp", "role"),
        P("role", "tp"),
        P("role", "tp"),
        P("role", "tp"),
        P("tp", "role"),
        P("role", "tp"),
    )
    return jax.shard_map(
        on_device,
        mesh=mesh,
        in_specs=placed,
        out_specs=(
            P(("groups", "role"), "tp"),
            P(("groups", "role"), "tp"),
            P(("groups", "tp"), "role"),
            P(("groups", "role"), "tp"),
        ),
        check_vma=False,
    )
```

profile of v0, /device:TPU:0, one launch (start us, length us, event | category | flops | bytes accessed | tf_op | source)
XLA Modules:
  0.0 431.9 jit_solution(6002679710210174196)
XLA Ops:
  8.1 1.2 copy-done
  9.2 7.2 %fusion.18 = f32[256,3584]{1,0:T(8,128)S(1)} fusion(bf16[256,2048]{1,0:T(8,128)(2,1)S(1)} %copy-done, bf16[2048,3584]{1,0:T(8,128)(2,1)} %param.12), kind=kOutput, calls=%fused_computation.29 | convolution fusion | flops 3758096384 | bytes 19398656 | tf_op jit(solution)/shard_map/dot_general | solution.py:49
  16.5 7.3 %fusion.17 = f32[256,3584]{1,0:T(8,128)S(1)} fusion(bf16[256,2048]{1,0:T(8,128)(2,1)S(1)} %copy-done, bf16[2048,3584]{1,0:T(8,128)(2,1)} %param.11), kind=kOutput, calls=%fused_computation.28 | convolution fusion | flops 3758096384 | bytes 19398656 | tf_op jit(solution)/shard_map/dot_general | solution.py:48
  23.8 3.4 pad_maximum_fusion
  28.3 4.9 %fusion.14 = f32[256,2048]{1,0:T(8,128)} fusion(bf16[256,1024]{1,0:T(8,128)(2,1)S(1)} %copy-done.7, bf16[1024,2048]{1,0:T(8,128)(2,1)} %param.14), kind=kOutput, calls=%fused_computation.25 | convolution fusion | flops 1073741824 | bytes 6815744 | tf_op jit(solution)/shard_map/dot_general | solution.py:60
  33.2 2.6 fusion.15
  35.9 122.1 %reduce-scatter.2.cloned.1.call-done = f32[64,7168]{1,0:T(8,128)} async-done(((f32[256,7168]{1,0:T(8,128)}), f32[64,7168]{1,0:T(8,128)}) %reduce-scatter.2.cloned.1.call-update) | async-done | bytes 1835024 | tf_op jit(solution)/shard_map/reduce_scatter | solution.py:30
  158.0 2.5 fusion.2
  160.6 3.0 multiply_convert_fusion.3
  164.0 1.3 fusion.16
  165.3 69.8 %all-reduce.12 = bf16[256,1024]{1,0:T(8,128)(2,1)S(1)} all-reduce(f32[256,1024]{1,0:T(8,128)S(1)} %fusion.16), channel_id=1, replica_groups=mesh['groups'=2,'role'=4,'tp'=4] {'tp'}, use_global_device_ids=true, to_apply=%region_2.3 | all-reduce | flops 262144 | bytes 1572864 | tf_op jit(solution)/shard_map/psum | solution.py:26
  235.1 7.9 %fusion.19 = f32[256,2048]{1,0:T(8,128)S(1)} fusion(bf16[256,3584]{1,0:T(8,128)(2,1)} %all-gather.2.cloned.1.call-done, bf16[3584,2048]{1,0:T(8,128)(2,1)} %param.13), kind=kOutput, calls=%fused_computation.30 | convolution fusion | flops 3758096384 | bytes 18612224 | tf_op jit(solution)/shard_map/dot_general | solution.py:53
  243.0 2.6 convolution_subtract_fusion
  245.9 51.1 %all-reduce.7.cloned.1.call-done = f32[256,2048]{1,0:T(8,128)} async-done(((f32[256,2048]{1,0:T(8,128)}), f32[256,2048]{1,0:T(8,128)}) %all-reduce.7.cloned.1.call-update) | async-done | bytes 2097168 | tf_op jit(solution)/shard_map/psum | solution.py:22
  297.0 4.1 fusion.3
  301.2 43.6 %all-reduce.13 = bf16[256,1024]{1,0:T(8,128)(2,1)S(1)} all-reduce(f32[256,1024]{1,0:T(8,128)S(1)} %fusion.3), channel_id=1, replica_groups=mesh['groups'=2,'role'=4,'tp'=4] {'tp'}, use_global_device_ids=true, to_apply=%region_5.6 | all-reduce | flops 262144 | bytes 1572864 | tf_op jit(solution)/shard_map/psum | solution.py:26
  344.8 4.8 %fusion.20 = f32[256,2048]{1,0:T(8,128)} fusion(bf16[256,1024]{1,0:T(8,128)(2,1)S(1)} %all-reduce.13, bf16[2048,1024]{1,0:T(8,128)(2,1)} %param.16), kind=kOutput, calls=%fused_computation.31 | convolution fusion | flops 1073741824 | bytes 6815744 | tf_op jit(solution)/shard_map/dot_general | solution.py:16
  349.6 3.3 convolution_convert_fusion.1
  352.9 3.3 convolution_convert_fusion
  356.2 43.1 %all-reduce.9.cloned.1.call-done = f32[256,2048]{1,0:T(8,128)} async-done(((f32[256,2048]{1,0:T(8,128)}), f32[256,2048]{1,0:T(8,128)}) %all-reduce.9.cloned.1.call-update) | async-done | bytes 2097168 | tf_op jit(solution)/shard_map/psum | solution.py:22
  399.3 7.0 %convert_bitcast_fusion.1 = bf16[1024,2048]{0,1:T(8,128)(2,1)} fusion(bf16[256,1024]{1,0:T(8,128)(2,1)S(1)} %copy-done.8, f32[256,2048]{1,0:T(8,128)} %get-tuple-element.8, f32[256,2048]{1,0:T(8,128)} %all-reduce.9.cloned.1.call-done, f32[256,2048]{1,0:T(8,128)} %get-tuple-element.9), kind=kOutput, calls=%fused_computation.2 | convolution fusion | flops 1081081856 | bytes 11010048 | tf_op jit(solution)/shard_map/dot_general | solution.py:10
  406.3 6.6 %copy.13 = bf16[1024,2048]{1,0:T(8,128)(2,1)} copy(bf16[1024,2048]{0,1:T(8,128)(2,1)} %convert_bitcast_fusion.1) | data formatting | bytes 8388608
  412.9 4.9 %convert_bitcast_fusion = bf16[1024,2048]{0,1:T(8,128)(2,1)} fusion(bf16[256,1024]{1,0:T(8,128)(2,1)S(1)} %copy-done.8, f32[256,2048]{1,0:T(8,128)} %all-reduce.9.cloned.1.call-done, f32[256,2048]{1,0:T(8,128)S(1)} %copy-done.4), kind=kOutput, calls=%fused_computation.1 | convolution fusion | flops 1078984704 | bytes 8912896 | tf_op jit(solution)/shard_map/dot_general | solution.py:10
  417.8 6.5 %copy.14 = bf16[1024,2048]{1,0:T(8,128)(2,1)} copy(bf16[1024,2048]{0,1:T(8,128)(2,1)} %convert_bitcast_fusion) | data formatting | bytes 8388608
  (29 shorter events, 2.0 us)
Async XLA Ops:
  8.0 1.2 copy-start
  8.0 150.0 %reduce-scatter.2.cloned.1.call-start = ((), (), s32[]{:S(2)}) async-start(), calls=%async_computation.1 | async-start | bytes 9175040 | tf_op jit(solution)/shard_map/reduce_scatter | solution.py:30
  27.2 1.0 copy-start.7
  27.3 133.3 %all-reduce.11.cloned.1.call-start = ((), (), s32[]{:S(2)}) async-start(), calls=%async_computation.5 | async-start | bytes 8388608 | tf_op jit(solution)/shard_map/psum | solution.py:22
  28.3 4.9 %copy-start.5 = (bf16[1024,2048]{1,0:T(8,128)(2,1)S(1)}, bf16[1024,2048]{1,0:T(8,128)(2,1)}, u32[]{:S(2)}) copy-start(bf16[1024,2048]{1,0:T(8,128)(2,1)} %param.15) | copy-start | bytes 12582916
  35.8 199.2 %all-gather.2.cloned.1.call-start = ((), (), s32[]{:S(2)}) async-start(), calls=%async_computation.2 | async-start | bytes 2293760 | tf_op jit(solution)/shard_map/all_gather | solution.py:39
  160.5 136.6 %all-reduce.7.cloned.1.call-start = ((), (), s32[]{:S(2)}) async-start(), calls=%async_computation.3 | async-start | bytes 4194304 | tf_op jit(solution)/shard_map/psum | solution.py:22
  160.5 3.5 copy-start.6
  235.1 8.0 %copy-start.2 = (bf16[1024,2048]{1,0:T(8,128)(2,1)S(1)}, bf16[1024,2048]{1,0:T(8,128)(2,1)}, u32[]{:S(2)}) copy-start(bf16[1024,2048]{1,0:T(8,128)(2,1)} %param.17) | copy-start | bytes 12582916
  245.7 153.6 %all-reduce.9.cloned.1.call-start = ((), (), s32[]{:S(2)}) async-start(), calls=%async_computation.4 | async-start | bytes 4194304 | tf_op jit(solution)/shard_map/psum | solution.py:22
  349.6 3.3 copy-start.3
  352.9 46.4 %copy-start.8 = (bf16[256,1024]{1,0:T(8,128)(2,1)S(1)}, bf16[256,1024]{1,0:T(8,128)(2,1)}, u32[]{:S(2)}) copy-start(bf16[256,1024]{1,0:T(8,128)(2,1)} %param.10) | copy-start | bytes 1572868
  406.3 6.6 %copy-start.4 = (f32[256,2048]{1,0:T(8,128)S(1)}, f32[256,2048]{1,0:T(8,128)}, u32[]{:S(2)}) copy-start(f32[256,2048]{1,0:T(8,128)} %get-tuple-element.8) | copy-start | bytes 6291460
  417.8 6.5 %copy-start.1 = (bf16[256,2048]{1,0:T(8,128)(2,1)S(1)}, bf16[256,2048]{1,0:T(8,128)(2,1)}, u32[]{:S(2)}) copy-start(bf16[256,2048]{1,0:T(8,128)(2,1)} %param.9) | copy-start | bytes 3145732
Sparse Core Ops, SparseCore 0:
  27.4 130.5 reduce-scatter.1
  160.6 69.2 all-gather.1
Sparse Core Ops, SparseCore 1:
  35.9 88.1 all-reduce.10
  245.8 51.2 all-reduce.6
  349.7 49.6 all-reduce.8
where the time goes:
time: 432 us
  waiting for transfers between devices  216 us (50%)
  blocking collectives  113 us (26%)
  matrix products  61.3 us (14%)
  between operations  15.8 us (4%)
  local copies, waits for them, and re-layouts  15.7 us (4%)
  other arithmetic  8.9 us (2%)
    reduce_scatter x1, waiting for transfers between devices, tp_scatter(): lax.psum_scatter(term_fn(jnp.int32(0), lax.axis_size('tp') * share_rows),...  122 us
    psum x2, blocking collectives, tp_sums(): return lax.psum(values, 'tp')  113 us
    psum x3, waiting for transfers between devices, role_sums(): return lax.psum(values, 'role')  94.2 us
    dot_general x4, matrix products, contract_rows(): lax.dot_general(left, right, (((0,), (0,)), ((), ())), preferred_element_...  18.5 us
    unnamed x20, local copies, waits for them, and re-layouts  15.7 us
    dot_general x2, matrix products, contract_cols(): lax.dot_general(left, right, (((1,), (1,)), ((), ())), preferred_element_...  8.9 us
  transfers between devices with their start and end apart: 5, of which 3 were waited for; matrix products, arithmetic and copies ran while one was open for 5% of the time, Pallas kernels for 0%

commit v1 on v0

--- a/solution.py
+++ b/solution.py
@@ -4,6 +4,12 @@
 from jax.sharding import PartitionSpec as P
 
 loss_scale = 16.0
+
+
+def add_all(value, axis):
+    parts = lax.all_gather(value, axis, axis=0, tiled=False)
+    summed = parts.sum(axis=0)
+    return summed
 
 
 def contract_rows(left, right):
@@ -23,7 +29,7 @@
 
 
 def tp_sums(values):
-    return lax.psum(values, "tp")
+    return add_all(values, "tp")
 
 
 def tp_scatter(term_fn, share_rows):

time: 432 us -> 527 us (1.22)
  waiting for transfers between devices: 216 us -> 417 us
  blocking collectives: 113 us -> 0 us
  other arithmetic: 8.9 us -> 14.3 us
    all_gather x0 -> x2, waiting for transfers between devices: none -> 161 us  [add_all(): parts = lax.all_gather(value, axis, axis=0, tiled=False)]
    psum x2 -> x0, blocking collectives: 113 us -> none  [tp_sums(): return lax.psum(values, 'tp')]
    reduce_scatter x1, waiting for transfers between devices: 122 us -> 54.5 us  [tp_scatter(): lax.psum_scatter(term_fn(jnp.int32(0), lax.axis_size('tp') * share_rows),...]
    psum x3, waiting for transfers between devices: 94.2 us -> 161 us  [role_sums(): return lax.psum(values, 'role')]
    all_gather x1, waiting for transfers between devices: 0.02 us -> 39 us  [tp_gather(): lax.all_gather(shares, 'tp', axis=0, tiled=True)]
    reduce_sum x0 -> x2, other arithmetic: none -> 5.39 us  [add_all(): summed = parts.sum(axis=0)]
    unnamed x20 -> x18, local copies, waits for them, and re-layouts: 15.7 us -> 13.6 us
  transfers between devices with their start and end apart: 5 -> 7, of which waited for: 3 -> 7; matrix products, arithmetic and copies ran while one was open for 5% -> 7% of each run, Pallas kernels for 0% -> 0%
where the time goes in v1:
time: 527 us; the launch traced here: 526 us
  waiting for transfers between devices  417 us (79%)
  matrix products  65.7 us (12%)
  between operations  15.6 us (3%)
  other arithmetic  14.3 us (3%)
  local copies, waits for them, and re-layouts  13.6 us (3%)
    psum x3, waiting for transfers between devices, role_sums(): return lax.psum(values, 'role')  161 us
    all_gather x2, waiting for transfers between devices, add_all(): parts = lax.all_gather(value, axis, axis=0, tiled=False)  161 us
    reduce_scatter x1, waiting for transfers between devices, tp_scatter(): lax.psum_scatter(term_fn(jnp.int32(0), lax.axis_size('tp') * share_rows),...  54.5 us
    all_gather x1, waiting for transfers between devices, tp_gather(): lax.all_gather(shares, 'tp', axis=0, tiled=True)  39 us
    dot_general x4, matrix products, contract_rows(): lax.dot_general(left, right, (((0,), (0,)), ((), ())), preferred_element_...  20.1 us
    unnamed x18, local copies, waits for them, and re-layouts  13.6 us
  transfers between devices with their start and end apart: 7, of which 7 were waited for; matrix products, arithmetic and copies ran while one was open for 7% of the time, Pallas kernels for 0%

profile of v1, /device:TPU:0, one launch (start us, length us, event | category | flops | bytes accessed | tf_op | source)
XLA Modules:
  0.0 526.1 jit_solution(7959304496718467282)
XLA Ops:
  8.1 5.1 fusion.14
  15.9 7.3 %fusion.18 = f32[256,3584]{1,0:T(8,128)S(1)} fusion(bf16[256,2048]{1,0:T(8,128)(2,1)S(1)} %copy-done, bf16[2048,3584]{1,0:T(8,128)(2,1)} %param.12), kind=kOutput, calls=%fused_computation.29 | convolution fusion | flops 3758096384 | bytes 19398656 | tf_op jit(solution)/shard_map/dot_general | solution.py:55
  23.1 8.0 %fusion.17 = f32[256,3584]{1,0:T(8,128)S(1)} fusion(bf16[256,2048]{1,0:T(8,128)(2,1)S(1)} %copy-done, bf16[2048,3584]{1,0:T(8,128)(2,1)} %param.11), kind=kOutput, calls=%fused_computation.28 | convolution fusion | flops 3758096384 | bytes 19398656 | tf_op jit(solution)/shard_map/dot_general | solution.py:54
  31.1 3.4 pad_maximum_fusion
  34.6 69.5 %all-reduce.9.cloned.1.call-done = (f32[256,2048]{1,0:T(8,128)}, f32[256,2048]{1,0:T(8,128)}) async-done(((f32[256,2048]{1,0:T(8,128)}, f32[256,2048]{1,0:T(8,128)}), (f32[256,2048]{1,0:T(8,128)}, f32[256,2048]{1,0:T(8,128)})) %all-reduce.9.cloned.1.call-update) | async-done | bytes 4194320 | tf_op jit(solution)/shard_map/psum | solution.py:28
  104.2 3.0 multiply_convert_fusion.3
  110.0 54.5 %reduce-scatter.2.cloned.1.call-done = f32[64,7168]{1,0:T(8,128)} async-done(((f32[256,7168]{1,0:T(8,128)}), f32[64,7168]{1,0:T(8,128)}) %reduce-scatter.2.cloned.1.call-update) | async-done | bytes 1835024 | tf_op jit(solution)/shard_map/reduce_scatter | solution.py:36
  167.0 80.6 %all-gather.8.cloned.1.call-done = f32[1024,1024]{1,0:T(8,128)} async-done(((f32[256,1024]{1,0:T(8,128)}), f32[1024,1024]{1,0:T(8,128)}) %all-gather.8.cloned.1.call-update) | async-done | bytes 4194320 | tf_op jit(solution)/shard_map/all_gather | solution.py:10
  247.7 2.7 reduce_sum.18
  250.3 39.0 %all-gather.6.cloned.1.call-done = bf16[256,3584]{1,0:T(8,128)(2,1)} async-done(((bf16[64,3584]{1,0:T(8,128)(2,1)}), bf16[256,3584]{1,0:T(8,128)(2,1)}) %all-gather.6.cloned.1.call-update) | async-done | bytes 1835024 | tf_op jit(solution)/shard_map/all_gather | solution.py:45
  289.4 7.9 %fusion.19 = f32[256,2048]{1,0:T(8,128)S(1)} fusion(bf16[256,3584]{1,0:T(8,128)(2,1)} %all-gather.6.cloned.1.call-done, bf16[3584,2048]{1,0:T(8,128)(2,1)} %param.13), kind=kOutput, calls=%fused_computation.30 | convolution fusion | flops 3758096384 | bytes 18612224 | tf_op jit(solution)/shard_map/dot_general | solution.py:59
  297.3 2.6 convolution_subtract_fusion
  300.2 50.1 %all-reduce.5.cloned.1.call-done = f32[256,2048]{1,0:T(8,128)} async-done(((f32[256,2048]{1,0:T(8,128)}), f32[256,2048]{1,0:T(8,128)}) %all-reduce.5.cloned.1.call-update) | async-done | bytes 2097168 | tf_op jit(solution)/shard_map/psum | solution.py:28
  350.3 5.1 fusion.3
  355.5 80.7 %all-gather.10.cloned.1.call-done = f32[1024,1024]{1,0:T(8,128)} async-done(((f32[256,1024]{1,0:T(8,128)}), f32[1024,1024]{1,0:T(8,128)}) %all-gather.10.cloned.1.call-update) | async-done | bytes 4194320 | tf_op jit(solution)/shard_map/all_gather | solution.py:10
  436.2 2.7 reduce_sum.19
  438.9 4.8 fusion.20
  443.7 4.9 convolution_convert_fusion
  448.6 3.3 convolution_convert_fusion.1
  451.9 41.8 %all-reduce.7.cloned.1.call-done = f32[256,2048]{1,0:T(8,128)} async-done(((f32[256,2048]{1,0:T(8,128)}), f32[256,2048]{1,0:T(8,128)}) %all-reduce.7.cloned.1.call-update) | async-done | bytes 2097168 | tf_op jit(solution)/shard_map/psum | solution.py:28
  493.7 7.0 %convert_bitcast_fusion.1 = bf16[1024,2048]{0,1:T(8,128)(2,1)} fusion(bf16[256,1024]{1,0:T(8,128)(2,1)S(1)} %copy-done.6, f32[256,2048]{1,0:T(8,128)} %get-tuple-element.8, f32[256,2048]{1,0:T(8,128)} %all-reduce.7.cloned.1.call-done, f32[256,2048]{1,0:T(8,128)} %get-tuple-element.9), kind=kOutput, calls=%fused_computation.2 | convolution fusion | flops 1081081856 | bytes 11010048 | tf_op jit(solution)/shard_map/dot_general | solution.py:16
  500.7 6.6 %copy.13 = bf16[1024,2048]{1,0:T(8,128)(2,1)} copy(bf16[1024,2048]{0,1:T(8,128)(2,1)} %convert_bitcast_fusion.1) | data formatting | bytes 8388608
  507.3 4.9 convert_bitcast_fusion
  512.2 6.5 %copy.14 = bf16[1024,2048]{1,0:T(8,128)(2,1)} copy(bf16[1024,2048]{0,1:T(8,128)(2,1)} %convert_bitcast_fusion) | data formatting | bytes 8388608
  (33 shorter events, 8.4 us)
Async XLA Ops:
  8.0 7.8 %copy-start = (bf16[256,2048]{1,0:T(8,128)(2,1)S(1)}, bf16[256,2048]{1,0:T(8,128)(2,1)}, u32[]{:S(2)}) copy-start(bf16[256,2048]{1,0:T(8,128)(2,1)} %param.9) | copy-start | bytes 3145732
  8.0 5.1 copy-start.6
  8.0 96.2 %all-reduce.9.cloned.1.call-start = ((), (), s32[]{:S(2)}) async-start(), calls=%async_computation.7 | async-start | bytes 8388608 | tf_op jit(solution)/shard_map/psum | solution.py:28
  8.1 5.1 copy-start.4
  15.8 148.7 %reduce-scatter.2.cloned.1.call-start = ((), (), s32[]{:S(2)}) async-start(), calls=%async_computation.1 | async-start | bytes 9175040 | tf_op jit(solution)/shard_map/reduce_scatter | solution.py:36
  34.6 213.1 %all-gather.8.cloned.1.call-start = ((), (), s32[]{:S(2)}) async-start(), calls=%async_computation.5 | async-start | bytes 5242880 | tf_op jit(solution)/shard_map/all_gather | solution.py:10
  104.2 3.4 copy-start.5
  109.9 179.5 %all-gather.6.cloned.1.call-start = ((), (), s32[]{:S(2)}) async-start(), calls=%async_computation.2 | async-start | bytes 2293760 | tf_op jit(solution)/shard_map/all_gather | solution.py:45
  167.0 183.3 %all-reduce.5.cloned.1.call-start = ((), (), s32[]{:S(2)}) async-start(), calls=%async_computation.3 | async-start | bytes 4194304 | tf_op jit(solution)/shard_map/psum | solution.py:28
  289.4 7.9 %copy-start.2 = (bf16[1024,2048]{1,0:T(8,128)(2,1)S(1)}, bf16[1024,2048]{1,0:T(8,128)(2,1)}, u32[]{:S(2)}) copy-start(bf16[1024,2048]{1,0:T(8,128)(2,1)} %param.17) | copy-start | bytes 12582916
  300.0 136.2 %all-gather.10.cloned.1.call-start = ((), (), s32[]{:S(2)}) async-start(), calls=%async_computation.6 | async-start | bytes 5242880 | tf_op jit(solution)/shard_map/all_gather | solution.py:10
  355.4 138.3 %all-reduce.7.cloned.1.call-start = ((), (), s32[]{:S(2)}) async-start(), calls=%async_computation.4 | async-start | bytes 4194304 | tf_op jit(solution)/shard_map/psum | solution.py:28
  500.7 6.6 %copy-start.3 = (f32[256,2048]{1,0:T(8,128)S(1)}, f32[256,2048]{1,0:T(8,128)}, u32[]{:S(2)}) copy-start(f32[256,2048]{1,0:T(8,128)} %get-tuple-element.8) | copy-start | bytes 6291460
  500.7 6.6 %copy-start.7 = (bf16[256,1024]{1,0:T(8,128)(2,1)S(1)}, bf16[256,1024]{1,0:T(8,128)(2,1)}, u32[]{:S(2)}) copy-start(bf16[256,1024]{1,0:T(8,128)(2,1)} %param.10) | copy-start | bytes 1572868
  512.2 6.5 %copy-start.1 = (bf16[256,2048]{1,0:T(8,128)(2,1)S(1)}, bf16[256,2048]{1,0:T(8,128)(2,1)}, u32[]{:S(2)}) copy-start(bf16[256,2048]{1,0:T(8,128)(2,1)} %param.9) | copy-start | bytes 3145732
Sparse Core Ops, SparseCore 0:
  15.9 88.2 all-reduce.8
  300.1 50.1 all-reduce.4
  443.8 49.8 all-reduce.6
Sparse Core Ops, SparseCore 1:
  34.7 129.8 reduce-scatter.1
  166.5 81.1 all-gather.7
  249.7 39.7 all-gather.5
  355.5 80.6 all-gather.9
